TPU v7x, 512 devices: a whole 4x4x16 slice. The times are simulated.
512 devices in a mesh: tm: 16 (over z), expert: 32 (over x, y, core).
Axes of the slice: x: 4, y: 4, z: 16, core: 2. Of those that a mesh axis runs over, the one named last changes fastest.
Arguments:
- x_in: float32 [32, 4096, 1024], P('expert', 'tm'), may hold values from -6 to 6
- z_gate: bfloat16 [32, 4096, 1024], P('expert', 'tm'), may hold values from -6 to 6
- b_proj: float32 [32, 4096, 128], P('expert', 'tm'), may hold values from -1.5 to 1.5
- c_proj: float32 [32, 4096, 128], P('expert', 'tm'), may hold values from -1.5 to 1.5
- decay_log: float32 [32, 4096, 16], P('expert', 'tm'), as said below
- skip_gain: float32 [16], replicated, may hold values from 0.5 to 2
- residual: float32 [32, 4096, 1024], P('expert', 'tm'), may hold values from -6 to 6
- ssd_gain: float32 [1024], replicated, may hold values from 0.5 to 1.5
- moe_gain: float32 [1024], replicated, may hold values from 0.5 to 1.5
- w_gate: bfloat16 [32, 1024, 1536], P('expert', 'tm'), may hold values from -0.1875 to 0.1875
- w_up: bfloat16 [32, 1024, 1536], P('expert', 'tm'), may hold values from -0.1875 to 0.1875
- w_down: bfloat16 [32, 1536, 1024], P('expert', 'tm'), may hold values from -0.15625 to 0.15625
- routes: int32 [32, 4096, 2], P('expert', 'tm'), may hold values from 0 to 31, all different within a row; in each aligned block of 256 rows (0 to 255, 256 to 511, ..., all dimensions but the last counted through in order) at most 24 rows name the same one
- route_weights: float32 [32, 4096, 2], P('expert', 'tm'), may hold values from 0.2 to 1
Outputs:
- mixed: float32 [32, 4096, 1024], P('expert', 'tm')
Inputs may be any that keep to these rules, and one draw needn't show every extreme that they name: `routes`: the two experts of a time step differ. Among the time steps of one device no expert is named more than 24 times, and in every draw some device names some expert exactly 24 times. `decay_log`: every entry is at most zero.
All inputs are finite; a program needn't handle non-finite values.
Results may differ from a plain program's by a relative error of at most 0.0021.
Values may be sent and summed in bfloat16 or wider, within the bound.
No kernel may reach another device: no remote copies, remote signals or barrier semaphores. Data moves between devices by JAX's collectives and lax.ppermute only.
A program may use at most 64 MiB of HBM per device.

v0:
```python
import math
import jax
import jax.numpy as jnp
from jax import lax
from jax.sharding import PartitionSpec as P

exact_mode = lax.Precision.HIGHEST


def carried_in_2(value, axis, join, neutral):
    count, mine = (lax.axis_size(axis), lax.axis_index(axis))
    pieces = jax.tree.map(lambda part: lax.all_gather(part, axis), value)
    running = jax.tree.map(
        lambda part, zero: jnp.full_like(part, 0) + jnp.asarray(zero, part.dtype), value, neutral
    )

    def lap(position, running):
        longer = join(running, jax.tree.map(lambda part: part[position], pieces))
        return jax.tree.map(lambda new, old: jnp.where(position < mine, new, old), longer, running)

    return lax.fori_loop(0, count - 1, lap, running)


def group_carry(state, values, b_rows, running):
    remains = jnp.exp(running[-1][None, :] - running)
    fresh = jnp.einsum("jhp,jn->hpn", values * remains[:, :, None], b_rows, precision=exact_mode)
    return jnp.exp(running[-1])[:, None, None] * state + fresh


def group_step(state, inputs, skip_gain):
    values, b_rows, c_rows, log_rates = inputs
    length = values.shape[0]
    running = jnp.cumsum(log_rates, axis=0)
    across = running.T[:, :, None] - running.T[:, None, :]
    places = jnp.arange(length)
    causal = (places[:, None] >= places[None, :])[None]
    masked = jnp.where(causal, jnp.exp(jnp.where(causal, across, 0.0)), 0.0)
    scores = jnp.dot(c_rows, b_rows.T, precision=exact_mode)
    mixing = masked * scores[None]
    output = jnp.einsum("hij,jhp->ihp", mixing, values, precision=exact_mode)
    output = output + jnp.exp(running)[:, :, None] * jnp.einsum(
        "in,hpn->ihp", c_rows, state, precision=exact_mode
    )
    output = output + skip_gain[None, :, None] * values
    return (group_carry(state, values, b_rows, running), output)


def incoming_state(through, local_end):

    def combine(earlier, later):
        return (earlier[0] * later[0], later[0][:, None, None] * earlier[1] + later[1])

    prefix = carried_in_2(
        (through, local_end), "tm", combine, (jnp.ones_like(through), jnp.zeros_like(local_end))
    )
    return prefix[1]


def rms_scale(rows, gain):
    return gain * rows / jnp.sqrt(jnp.mean(rows * rows, axis=-1, keepdims=True) + 1e-05)


def per_device(
    x_in,
    z_gate,
    b_proj,
    c_proj,
    decay_log,
    skip_gain,
    residual,
    ssd_gain,
    moe_gain,
    w_gate,
    w_up,
    w_down,
    routes,
    route_weights,
):
    heads = skip_gain.shape[0]
    model_width = x_in.shape[2]
    width = model_width // heads
    length = x_in.shape[1]
    block = math.gcd(length, 256)
    count = length // block
    values = x_in[0].reshape(length, heads, width)
    b_rows = b_proj[0]
    c_rows = c_proj[0]
    log_rates = decay_log[0]
    inputs = (
        values.reshape(count, block, heads, width),
        b_rows.reshape(count, block, -1),
        c_rows.reshape(count, block, -1),
        log_rates.reshape(count, block, heads),
    )
    start = jnp.zeros((heads, width, b_rows.shape[1]), jnp.float32)
    through = jnp.exp(jnp.sum(log_rates, axis=0))
    local_end, outputs = lax.scan(
        lambda state, piece: group_step(state, piece, skip_gain), start, inputs
    )
    incoming = incoming_state(through, local_end)
    running = jnp.cumsum(log_rates, axis=0)
    carried_in = jnp.exp(running)[:, :, None] * jnp.einsum(
        "in,hpn->ihp", c_rows, incoming, precision=exact_mode
    )
    mixed_ssd = (outputs.reshape(length, heads, width) + carried_in).reshape(length, model_width)
    gated = mixed_ssd * jax.nn.silu(z_gate[0].astype(jnp.float32))
    hres = residual[0] + rms_scale(gated, ssd_gain)
    normed = rms_scale(hres, moe_gain).astype(jnp.bfloat16)
    expert_count = lax.axis_size("expert")
    capacity = max(2, 3 * length // expert_count)
    flat_routes = routes[0].reshape(-1)
    picked_one = (flat_routes[:, None] == jnp.arange(expert_count)[None, :]).astype(jnp.int32)
    earlier_hits = jnp.cumsum(picked_one, axis=0) - picked_one
    slot_index = jnp.sum(earlier_hits * picked_one, axis=1)
    target = flat_routes * capacity + slot_index
    repeated = jnp.broadcast_to(normed[:, None, :], (length, 2, model_width)).reshape(
        2 * length, model_width
    )
    outgoing = (
        jnp.zeros((expert_count * capacity, model_width), jnp.bfloat16).at[target].set(repeated)
    )
    received = lax.all_to_all(
        outgoing.reshape(expert_count, capacity, model_width),
        "expert",
        split_axis=0,
        concat_axis=0,
        tiled=True,
    )
    received = received.reshape(expert_count * capacity, model_width)
    slot_rows = expert_count * capacity
    columns = received
    gate = jnp.dot(
        columns,
        lax.all_gather(w_gate[0], "tm", axis=0, tiled=True),
        preferred_element_type=jnp.float32,
    )
    upper = jnp.dot(
        columns,
        lax.all_gather(w_up[0], "tm", axis=0, tiled=True),
        preferred_element_type=jnp.float32,
    )
    hidden = (jax.nn.silu(gate) * upper).astype(jnp.bfloat16)
    columns = hidden
    produced = jnp.dot(
        columns,
        lax.all_gather(w_down[0], "tm", axis=0, tiled=True),
        preferred_element_type=jnp.float32,
    ).astype(jnp.bfloat16)
    back = lax.all_to_all(
        produced.reshape(expert_count, capacity, model_width),
        "expert",
        split_axis=0,
        concat_axis=0,
        tiled=True,
    )
    back = back.reshape(slot_rows, model_width)
    fetched = back[target].astype(jnp.float32).reshape(length, 2, model_width)
    weights_here = route_weights[0]
    moe = fetched[:, 0, :] * weights_here[:, 0:1] + fetched[:, 1, :] * weights_here[:, 1:2]
    return (hres + moe).reshape(1, length, model_width)


def solution(mesh):
    in_specs = (
        P("expert", "tm", None),
        P("expert", "tm", None),
        P("expert", "tm", None),
        P("expert", "tm", None),
        P("expert", "tm", None),
        P(),
        P("expert", "tm", None),
        P(),
        P(),
        P("expert", "tm", None),
        P("expert", "tm", None),
        P("expert", "tm", None),
        P("expert", "tm", None),
        P("expert", "tm", None),
    )
    out_specs = P("expert", "tm", None)
    return jax.shard_map(
        per_device, mesh=mesh, in_specs=in_specs, out_specs=out_specs, check_vma=False
    )
```

profile of v0, /device:TPU:1, one launch (start us, length us, event | category | flops | bytes accessed | tf_op | source)
XLA Modules:
  0.0 405.9 jit_solution(9429766804105325587)
XLA Ops:
  8.5 1.6 copy.54
  10.2 1.8 convolution_add_fusion
  17.1 32.2 %all-reduce = f32[256]{0:T(256)S(1)} all-reduce(f32[256]{0:T(256)S(1)} %exponential_dynamic-update-slice_fusion), channel_id=2, replica_groups=mesh['tm'=16,'expert'=32] {'tm'}, use_global_device_ids=true, to_apply=%add | all-reduce | flops 256 | bytes 2048
  52.4 5.1 %fusion.24 = f32[256,16,64]{0,2,1:T(8,128)S(1)} fusion(f32[256,16,64]{0,2,1:T(8,128)S(1)} %bitcast.161, f32[256,256]{1,0:T(8,128)S(1)} %fusion.49, f32[16,256]{1,0:T(8,128)S(1)} %get-tuple-element.159, pred[256,256]{1,0:T(8,128)(4,1)S(1)} %iota_compare_fusion), kind=kOutput, calls=%fused_computation.23 | convolution fusion | flops 809500672 | bytes 2441216 | tf_op jit(solution)/shard_map/while/body/eval_jaxpr/hij,jhp->ihp/dot_general | solution.py:40
  57.6 2.1 fusion.31
  59.7 64.1 %all-gather.10.cloned.1.call-done = f32[256,64,128]{2,1,0:T(8,128)} async-done(((f32[16,64,128]{2,1,0:T(8,128)}), f32[256,64,128]{2,1,0:T(8,128)}) %all-gather.10.cloned.1.call-update) | async-done | bytes 8388624 | tf_op jit(solution)/shard_map/all_gather | solution.py:12
  123.7 18.2 %while.9 = (s32[]{:T(128)}, f32[16,64,128]{2,1,0:T(8,128)S(1)}, s32[]{:T(128)}, f32[16,16]{1,0:T(8,128)S(1)}, f32[16,16,64,128]{3,2,1,0:T(8,128)}, /*index=5*/s32[]{:T(128)}, s32[]{:T(128)}) while((s32[]{:T(128)}, f32[16,64,128]{2,1,0:T(8,128)S(1)}, s32[]{:T(128)}, f32[16,16]{1,0:T(8,128)S(1)}, f32[16,16,64,128]{3,2,1,0:T(8,128)}, ...), condition=%wide.region_4.5_spmd.clone, body=%wide.region_3.4_spmd.clone.sunk | while | flops 524292 | bytes 1573161 | solution.py:21
  142.0 2.8 multiply_reduce_fusion.1
  144.8 1.3 copy.62
  146.1 1.8 multiply_reduce_fusion
  149.9 4.5 %scatter_custom_fusion = bf16[768,1024]{1,0:T(8,128)(2,1)} fusion(s32[512]{0:T(512)S(1)} %bitcast.171, bf16[512,1024]{1,0:T(8,128)(2,1)} %reshape.351, bf16[]{:T(256)} %constant.72.clone.1), kind=kCustom, calls=%fused_computation.51 | custom fusion | bytes 1573376 | tf_op jit(solution)/shard_map/scatter | solution.py:120
  154.4 7.5 %all-to-all-start = ((bf16[32,24,1024]{2,1,0:T(8,128)(2,1)}), bf16[32,24,1024]{2,1,0:T(8,128)(2,1)S(1)}, u32[]{:S(2)}, u32[]{:S(2)}) async-start(bf16[32,24,1024]{2,1,0:T(8,128)(2,1)} %bitcast.23), calls=%async_computation | async-start | bytes 3145728 | tf_op jit(solution)/shard_map/all_to_all | solution.py:122
  162.0 29.4 %all-gather.12.cloned.1.call-done = bf16[1,1024,1536]{2,1,0:T(8,128)(2,1)} async-done(((bf16[1,64,1536]{2,1,0:T(8,128)(2,1)}), bf16[1,1024,1536]{2,1,0:T(8,128)(2,1)}) %all-gather.12.cloned.1.call-update) | async-done | bytes 3145744 | tf_op jit(solution)/shard_map/all_gather | solution.py:134
  191.3 6.1 %fusion.10 = f32[768,1536]{1,0:T(8,128)} fusion(bf16[768,1024]{1,0:T(8,128)(2,1)S(1)} %bitcast.166, bf16[1,1024,1536]{2,1,0:T(8,128)(2,1)} %all-gather.12.cloned.1.call-done), kind=kOutput, calls=%fused_computation.15 | convolution fusion | flops 2415919104 | bytes 9437184 | tf_op jit(solution)/shard_map/dot_general | solution.py:132
  197.4 69.0 %all-gather.14.cloned.1.call-done = bf16[1,1024,1536]{2,1,0:T(8,128)(2,1)} async-done(((bf16[1,64,1536]{2,1,0:T(8,128)(2,1)}), bf16[1,1024,1536]{2,1,0:T(8,128)(2,1)}) %all-gather.14.cloned.1.call-update) | async-done | bytes 3145744 | tf_op jit(solution)/shard_map/all_gather | solution.py:139
  266.4 75.2 %all-gather.16.cloned.1.call-done = bf16[1,1536,1024]{2,1,0:T(8,128)(2,1)} async-done(((bf16[1,96,1024]{2,1,0:T(8,128)(2,1)}), bf16[1,1536,1024]{2,1,0:T(8,128)(2,1)}) %all-gather.16.cloned.1.call-update) | async-done | bytes 3145744 | tf_op jit(solution)/shard_map/all_gather | solution.py:146
  341.6 10.5 %fusion.19 = bf16[768,1024]{1,0:T(8,128)(2,1)} fusion(bf16[1,1536,1024]{2,1,0:T(8,128)(2,1)} %all-gather.16.cloned.1.call-done, f32[768,1536]{1,0:T(8,128)} %fusion.10, bf16[768,1024]{1,0:T(8,128)(2,1)S(1)} %bitcast.167, bf16[1,1024,1536]{2,1,0:T(8,128)(2,1)} %all-gather.14.cloned.1.call-done), kind=kOutput, calls=%fused_computation.22 | convolution fusion | flops 4839702528 | bytes 14155776 | tf_op jit(solution)/shard_map/dot_general | solution.py:144
  352.0 16.2 %all-to-all-start.1 = ((bf16[32,24,1024]{2,1,0:T(8,128)(2,1)}), bf16[32,24,1024]{2,1,0:T(8,128)(2,1)S(1)}, u32[]{:S(2)}, u32[]{:S(2)}) async-start(bf16[32,24,1024]{2,1,0:T(8,128)(2,1)} %bitcast.168), calls=%async_computation.1 | async-start | bytes 3145728 | tf_op jit(solution)/shard_map/all_to_all | solution.py:149
  368.3 1.3 copy.56
  369.6 21.3 %all-to-all-done.1 = bf16[32,24,1024]{2,1,0:T(8,128)(2,1)S(1)} async-done(((bf16[32,24,1024]{2,1,0:T(8,128)(2,1)}), bf16[32,24,1024]{2,1,0:T(8,128)(2,1)S(1)}, u32[]{:S(2)}, u32[]{:S(2)}) %all-to-all-start.1) | async-done | bytes 1572896 | tf_op jit(solution)/shard_map/all_to_all | solution.py:149
  390.9 2.8 gather_fusion
  393.7 2.4 reshape.338
  396.1 1.6 fusion.61
  397.7 1.6 fusion.34
  (102 shorter events, 29.2 us)
Async XLA Ops:
  6.5 8.1 %copy-start = (f32[1,256,128]{2,1,0:T(8,128)S(1)}, f32[1,256,128]{2,1,0:T(8,128)}, u32[]{:S(2)}) copy-start(f32[1,256,128]{2,1,0:T(8,128)} %param.19) | copy-start | bytes 393220
  6.5 3.6 copy-start.5
  6.5 117.2 %all-gather.10.cloned.1.call-start = ((), (), s32[]{:S(2)}) async-start(), calls=%async_computation.2 | async-start | bytes 8912896 | tf_op jit(solution)/shard_map/all_gather | solution.py:12
  8.4 5.6 %copy-start.6 = (f32[1,256,16]{1,2,0:T(8,128)S(1)}, f32[1,256,16]{1,2,0:T(8,128)}, u32[]{:S(2)}) copy-start(f32[1,256,16]{1,2,0:T(8,128)} %param.20) | copy-start | bytes 49156
  8.5 5.7 %copy-start.8 = (s32[1,256,2]{1,2,0:T(2,128)S(1)}, s32[1,256,2]{1,2,0:T(2,128)}, u32[]{:S(2)}) copy-start(s32[1,256,2]{1,2,0:T(2,128)} %param.28) | copy-start | bytes 6148
  10.0 39.4 %copy-start.1 = (bf16[1,256,1024]{2,1,0:T(8,128)(2,1)S(1)}, bf16[1,256,1024]{2,1,0:T(8,128)(2,1)}, u32[]{:S(2)}) copy-start(bf16[1,256,1024]{2,1,0:T(8,128)(2,1)} %param.17) | copy-start | bytes 1572868
  12.0 179.4 %all-gather.12.cloned.1.call-start = ((), (), s32[]{:S(2)}) async-start(), calls=%async_computation.3 | async-start | bytes 3342336 | tf_op jit(solution)/shard_map/all_gather | solution.py:134
  12.7 253.7 %all-gather.14.cloned.1.call-start = ((), (), s32[]{:S(2)}) async-start(), calls=%async_computation.4 | async-start | bytes 3342336 | tf_op jit(solution)/shard_map/all_gather | solution.py:139
  13.4 328.1 %all-gather.16.cloned.1.call-start = ((), (), s32[]{:S(2)}) async-start(), calls=%async_computation.5 | async-start | bytes 3342336 | tf_op jit(solution)/shard_map/all_gather | solution.py:146
  52.4 5.1 %copy-start.11 = (f32[16]{0:T(128)S(1)}, f32[16]{0:T(128)}, u32[]{:S(2)}) copy-start(f32[16]{0:T(128)} %param.21) | copy-start | bytes 196
  142.0 4.2 %copy-start.3 = (f32[1,256,1024]{2,1,0:T(8,128)S(1)}, f32[1,256,1024]{2,1,0:T(8,128)}, u32[]{:S(2)}) copy-start(f32[1,256,1024]{2,1,0:T(8,128)} %param.22) | copy-start | bytes 3145732
  142.0 4.1 %copy-start.7 = (f32[1024]{0:T(1024)S(1)}, f32[1024]{0:T(1024)}, u32[]{:S(2)}) copy-start(f32[1024]{0:T(1024)} %param.23) | copy-start | bytes 12292
  144.8 3.1 copy-start.9
  154.4 36.9 %all-to-all-start = ((bf16[32,24,1024]{2,1,0:T(8,128)(2,1)}), bf16[32,24,1024]{2,1,0:T(8,128)(2,1)S(1)}, u32[]{:S(2)}, u32[]{:S(2)}) async-start(bf16[32,24,1024]{2,1,0:T(8,128)(2,1)} %bitcast.23), calls=%async_computation | async-start | bytes 3145728 | tf_op jit(solution)/shard_map/all_to_all | solution.py:122
  352.0 16.2 %copy-start.10 = (f32[1,256,2]{1,2,0:T(2,128)S(1)}, f32[1,256,2]{1,2,0:T(2,128)}, u32[]{:S(2)}) copy-start(f32[1,256,2]{1,2,0:T(2,128)} %param.29) | copy-start | bytes 6148
  352.0 38.9 %all-to-all-start.1 = ((bf16[32,24,1024]{2,1,0:T(8,128)(2,1)}), bf16[32,24,1024]{2,1,0:T(8,128)(2,1)S(1)}, u32[]{:S(2)}, u32[]{:S(2)}) async-start(bf16[32,24,1024]{2,1,0:T(8,128)(2,1)} %bitcast.168), calls=%async_computation.1 | async-start | bytes 3145728 | tf_op jit(solution)/shard_map/all_to_all | solution.py:149
  396.1 1.7 copy-start.2
  396.1 1.7 copy-start.4
Sparse Core Ops, SparseCore 0:
  12.1 111.6 all-gather.9
  125.8 65.4 all-gather.11
  193.4 72.9 all-gather.13
  268.3 73.2 all-gather.15
where the time goes:
time: 407 us; the launch traced here: 406 us
  waiting for transfers between devices  261 us (64%)
  blocking collectives  32.2 us (8%)
  matrix products  28.7 us (7%)
  starting transfers between devices  23.9 us (6%)
  other arithmetic  23.6 us (6%)
  local copies, waits for them, and re-layouts  22.1 us (5%)
  between operations  14.1 us (3%)
    all_gather x1, waiting for transfers between devices, per_device(): lax.all_gather(w_down[0], 'tm', axis=0, tiled=True)  75.2 us
    all_gather x1, waiting for transfers between devices, per_device(): lax.all_gather(w_up[0], 'tm', axis=0, tiled=True)  69 us
    all_gather x1, waiting for transfers between devices, carried_in_2(): pieces = jax.tree.map(lambda part: lax.all_gather(part, axis), value)  64.1 us
    unnamed x1, blocking collectives  32.2 us
    all_gather x1, waiting for transfers between devices, per_device(): lax.all_gather(w_gate[0], 'tm', axis=0, tiled=True)  29.4 us
    all_to_all x1, waiting for transfers between devices, per_device(): lax.all_to_all(produced.reshape(expert_count, capacity, model_width), 'ex...  21.3 us
    select_n x15, other arithmetic, lap(): jnp.where(position < mine, new, old)  17.6 us
    all_to_all x1, starting transfers between devices, per_device(): lax.all_to_all(produced.reshape(expert_count, capacity, model_width), 'ex...  16.2 us
  transfers between devices with their start and end apart: 6, of which 5 were waited for; matrix products, arithmetic and copies ran while one was open for 12% of the time, Pallas kernels for 0%

commit v1 on v0

--- a/solution.py
+++ b/solution.py
@@ -1,3 +1,4 @@
+import functools
 import math
 import jax
 import jax.numpy as jnp
@@ -5,6 +6,36 @@
 from jax.sharding import PartitionSpec as P
 
 exact_mode = lax.Precision.HIGHEST
+
+
+def supply_entries_in(x_local, mesh_dim):
+    base_arr = jax.lax.axis_size(mesh_dim)
+    p_next = jax.lax.axis_index(mesh_dim)
+    b_next, newest, parts_out = (base_arr, p_next, x_local.shape[0])
+    panels = [j0 * b_next if k == 0 else j0 for k, j0 in enumerate(x_local.shape)]
+    arr_next = jnp.zeros(panels, x_local.dtype)
+    x_now = lax.dynamic_update_slice_in_dim(arr_next, x_local, newest * parts_out, axis=0)
+    found_now = piece_next = x_local
+    for pp in range(1, b_next // 2 + 1):
+        v_now = range(b_next)
+        res = map(lambda k: (k, (k + 1) % b_next), v_now)
+        vec_out = list(res)
+        found_now = jax.lax.ppermute(found_now, axis_name=mesh_dim, perm=vec_out)
+        x_now = lax.dynamic_update_slice_in_dim(
+            x_now, found_now, (newest - pp) % b_next * parts_out, axis=0
+        )
+        if 2 * pp < b_next:
+            out_arr = range(b_next)
+            mid_arr = map(lambda k: (k, (k - 1) % b_next), out_arr)
+            ready = list(mid_arr)
+            piece_next = jax.lax.ppermute(piece_next, axis_name=mesh_dim, perm=ready)
+            x_now = lax.dynamic_update_slice_in_dim(
+                x_now, piece_next, (newest + pp) % b_next * parts_out, axis=0
+            )
+    return x_now
+
+
+part_squares = functools.partial(supply_entries_in, mesh_dim="tm")
 
 
 def carried_in_2(value, axis, join, neutral):
@@ -134,11 +165,7 @@
         lax.all_gather(w_gate[0], "tm", axis=0, tiled=True),
         preferred_element_type=jnp.float32,
     )
-    upper = jnp.dot(
-        columns,
-        lax.all_gather(w_up[0], "tm", axis=0, tiled=True),
-        preferred_element_type=jnp.float32,
-    )
+    upper = jnp.dot(columns, part_squares(w_up[0]), preferred_element_type=jnp.float32)
     hidden = (jax.nn.silu(gate) * upper).astype(jnp.bfloat16)
     columns = hidden
     produced = jnp.dot(

time: 407 us -> 356 us (0.87)
  waiting for transfers between devices: 261 us -> 135 us
  starting transfers between devices: 23.9 us -> 78.6 us
  local copies, waits for them, and re-layouts: 22.1 us -> 47 us
  blocking collectives: 32.2 us -> 24.1 us
    all_gather x1 -> x0, waiting for transfers between devices: 69 us -> none  [per_device(): lax.all_gather(w_up[0], 'tm', axis=0, tiled=True)]
    ppermute x0 -> x15, starting transfers between devices: none -> 54.8 us  [the longest x7 37.1 us: supply_entries_in(): piece_next = jax.lax.ppermute(piece_next, axis_name=mesh_dim, perm=ready)]
    all_gather x1, waiting for transfers between devices: 64.1 us -> 20 us  [carried_in_2(): pieces = jax.tree.map(lambda part: lax.all_gather(part, axis), value)]
    ppermute x0 -> x15, waiting for transfers between devices: none -> 31.4 us  [the longest x8 31.4 us: supply_entries_in(): found_now = jax.lax.ppermute(found_now, axis_name=mesh_dim, perm=vec_out)]
    all_gather x1, waiting for transfers between devices: 29.4 us -> 0.01 us  [per_device(): lax.all_gather(w_gate[0], 'tm', axis=0, tiled=True)]
    all_gather x1, waiting for transfers between devices: 75.2 us -> 62.8 us  [per_device(): lax.all_gather(w_down[0], 'tm', axis=0, tiled=True)]
    dynamic_update_slice x0 -> x16, local copies, waits for them, and re-layouts: none -> 11.1 us  [the longest x8 5.59 us: supply_entries_in(): lax.dynamic_update_slice_in_dim(x_now, found_now, (newest - pp) % b_next...]
    mul x15, local copies, waits for them, and re-layouts: 0.14 us -> 10.4 us  [combine(): later[0][:, None, None] * earlier[1] + later[1]]
  transfers between devices with their start and end apart: 6 -> 20, of which waited for: 5 -> 9; matrix products, arithmetic and copies ran while one was open for 12% -> 22% of each run, Pallas kernels for 0% -> 0%
where the time goes in v1:
time: 356 us; the launch traced here: 353 us
  waiting for transfers between devices  135 us (38%)
  starting transfers between devices  78.6 us (22%)
  local copies, waits for them, and re-layouts  47 us (13%)
  matrix products  29.7 us (8%)
  other arithmetic  24.1 us (7%)
  blocking collectives  24.1 us (7%)
  between operations  14.6 us (4%)
    all_gather x1, waiting for transfers between devices, per_device(): lax.all_gather(w_down[0], 'tm', axis=0, tiled=True)  62.8 us
    ppermute x7, starting transfers between devices, supply_entries_in(): piece_next = jax.lax.ppermute(piece_next, axis_name=mesh_dim, perm=ready)  37.1 us
    ppermute x8, waiting for transfers between devices, supply_entries_in(): found_now = jax.lax.ppermute(found_now, axis_name=mesh_dim, perm=vec_out)  31.4 us
    unnamed x1, blocking collectives  24.1 us
    all_to_all x1, waiting for transfers between devices, per_device(): lax.all_to_all(produced.reshape(expert_count, capacity, model_width), 'ex...  20.1 us
    all_gather x1, waiting for transfers between devices, carried_in_2(): pieces = jax.tree.map(lambda part: lax.all_gather(part, axis), value)  20 us
    ppermute x8, starting transfers between devices, supply_entries_in(): found_now = jax.lax.ppermute(found_now, axis_name=mesh_dim, perm=vec_out)  17.7 us
    select_n x15, other arithmetic, lap(): jnp.where(position < mine, new, old)  17.6 us
  transfers between devices with their start and end apart: 20, of which 9 were waited for; matrix products, arithmetic and copies ran while one was open for 22% of the time, Pallas kernels for 0%

profile of v1, /device:TPU:1, one launch (start us, length us, event | category | flops | bytes accessed | tf_op | source)
XLA Modules:
  0.0 353.5 jit_solution(11945313874773318110)
XLA Ops:
  12.8 4.4 %collective-permute-start = (bf16[64,1536]{1,0:T(8,128)(2,1)S(1)}, bf16[64,1536]{1,0:T(8,128)(2,1)S(1)}, u32[]{:S(2)}, u32[]{:S(2)}) collective-permute-start(bf16[64,1536]{1,0:T(8,128)(2,1)S(1)} %bitcast.167), channel_id=1, source_target_pairs={{0,32},{32,64},{64,96},{96,128},{128,160},{160,192},{192,224},{224... | collective-permute-start | bytes 589832 | tf_op jit(solution)/shard_map/ppermute | solution.py:23
  17.2 9.5 %collective-permute-start.1 = (bf16[64,1536]{1,0:T(8,128)(2,1)S(1)}, bf16[64,1536]{1,0:T(8,128)(2,1)S(1)}, u32[]{:S(2)}, u32[]{:S(2)}) collective-permute-start(bf16[64,1536]{1,0:T(8,128)(2,1)S(1)} %bitcast.168), channel_id=1, source_target_pairs={{0,480},{32,0},{64,32},{96,64},{128,96},{160,128},{192,160},{224,1... | collective-permute-start | bytes 589832 | tf_op jit(solution)/shard_map/ppermute | solution.py:31
  29.7 24.1 %all-reduce = f32[256]{0:T(256)S(1)} all-reduce(f32[256]{0:T(256)S(1)} %exponential_dynamic-update-slice_fusion), channel_id=2, replica_groups=mesh['tm'=16,'expert'=32] {'tm'}, use_global_device_ids=true, to_apply=%add | all-reduce | flops 256 | bytes 2048
  60.4 5.1 %fusion.19 = f32[256,16,64]{0,2,1:T(8,128)S(1)} fusion(f32[256,16,64]{0,2,1:T(8,128)S(1)} %bitcast.157, f32[256,256]{1,0:T(8,128)S(1)} %fusion.44, f32[16,256]{1,0:T(8,128)S(1)} %get-tuple-element.159, pred[256,256]{1,0:T(8,128)(4,1)S(1)} %iota_compare_fusion), kind=kOutput, calls=%fused_computation.22 | convolution fusion | flops 809500672 | bytes 2441216 | tf_op jit(solution)/shard_map/while/body/eval_jaxpr/hij,jhp->ihp/dot_general | solution.py:71
  70.1 4.6 %collective-permute-start.3 = (bf16[64,1536]{1,0:T(8,128)(2,1)S(1)}, bf16[64,1536]{1,0:T(8,128)(2,1)S(1)}, u32[]{:S(2)}, u32[]{:S(2)}) collective-permute-start(bf16[64,1536]{1,0:T(8,128)(2,1)S(1)} %collective-permute-done.1), channel_id=1, source_target_pairs={{0,480},{32,0},{64,32},{96,64},{128,96},{160,128},{192,160},{224,1... | collective-permute-start | bytes 589832 | tf_op jit(solution)/shard_map/ppermute | solution.py:31
  76.1 4.3 %collective-permute-done.2 = bf16[64,1536]{1,0:T(8,128)(2,1)S(1)} collective-permute-done((bf16[64,1536]{1,0:T(8,128)(2,1)S(1)}, bf16[64,1536]{1,0:T(8,128)(2,1)S(1)}, u32[]{:S(2)}, u32[]{:S(2)}) %collective-permute-start.2) | collective-permute-done | bytes 196640 | tf_op jit(solution)/shard_map/ppermute | solution.py:23
  82.3 4.6 %collective-permute-start.5 = (bf16[64,1536]{1,0:T(8,128)(2,1)S(1)}, bf16[64,1536]{1,0:T(8,128)(2,1)S(1)}, u32[]{:S(2)}, u32[]{:S(2)}) collective-permute-start(bf16[64,1536]{1,0:T(8,128)(2,1)S(1)} %collective-permute-done.3), channel_id=1, source_target_pairs={{0,480},{32,0},{64,32},{96,64},{128,96},{160,128},{192,160},{224,1... | collective-permute-start | bytes 589832 | tf_op jit(solution)/shard_map/ppermute | solution.py:31
  88.3 4.5 %collective-permute-done.4 = bf16[64,1536]{1,0:T(8,128)(2,1)S(1)} collective-permute-done((bf16[64,1536]{1,0:T(8,128)(2,1)S(1)}, bf16[64,1536]{1,0:T(8,128)(2,1)S(1)}, u32[]{:S(2)}, u32[]{:S(2)}) %collective-permute-start.4) | collective-permute-done | bytes 196640 | tf_op jit(solution)/shard_map/ppermute | solution.py:23
  94.7 4.6 %collective-permute-start.7 = (bf16[64,1536]{1,0:T(8,128)(2,1)S(1)}, bf16[64,1536]{1,0:T(8,128)(2,1)S(1)}, u32[]{:S(2)}, u32[]{:S(2)}) collective-permute-start(bf16[64,1536]{1,0:T(8,128)(2,1)S(1)} %collective-permute-done.5), channel_id=1, source_target_pairs={{0,480},{32,0},{64,32},{96,64},{128,96},{160,128},{192,160},{224,1... | collective-permute-start | bytes 589832 | tf_op jit(solution)/shard_map/ppermute | solution.py:31
  100.7 4.7 %collective-permute-done.6 = bf16[64,1536]{1,0:T(8,128)(2,1)S(1)} collective-permute-done((bf16[64,1536]{1,0:T(8,128)(2,1)S(1)}, bf16[64,1536]{1,0:T(8,128)(2,1)S(1)}, u32[]{:S(2)}, u32[]{:S(2)}) %collective-permute-start.6) | collective-permute-done | bytes 196640 | tf_op jit(solution)/shard_map/ppermute | solution.py:23
  107.4 4.6 %collective-permute-start.9 = (bf16[64,1536]{1,0:T(8,128)(2,1)S(1)}, bf16[64,1536]{1,0:T(8,128)(2,1)S(1)}, u32[]{:S(2)}, u32[]{:S(2)}) collective-permute-start(bf16[64,1536]{1,0:T(8,128)(2,1)S(1)} %collective-permute-done.7), channel_id=1, source_target_pairs={{0,480},{32,0},{64,32},{96,64},{128,96},{160,128},{192,160},{224,1... | collective-permute-start | bytes 589832 | tf_op jit(solution)/shard_map/ppermute | solution.py:31
  113.3 5.0 %collective-permute-done.8 = bf16[64,1536]{1,0:T(8,128)(2,1)S(1)} collective-permute-done((bf16[64,1536]{1,0:T(8,128)(2,1)S(1)}, bf16[64,1536]{1,0:T(8,128)(2,1)S(1)}, u32[]{:S(2)}, u32[]{:S(2)}) %collective-permute-start.8) | collective-permute-done | bytes 196640 | tf_op jit(solution)/shard_map/ppermute | solution.py:23
  120.3 4.8 %collective-permute-start.11 = (bf16[64,1536]{1,0:T(8,128)(2,1)S(1)}, bf16[64,1536]{1,0:T(8,128)(2,1)S(1)}, u32[]{:S(2)}, u32[]{:S(2)}) collective-permute-start(bf16[64,1536]{1,0:T(8,128)(2,1)S(1)} %collective-permute-done.9), channel_id=1, source_target_pairs={{0,480},{32,0},{64,32},{96,64},{128,96},{160,128},{192,160},{224,1... | collective-permute-start | bytes 589832 | tf_op jit(solution)/shard_map/ppermute | solution.py:31
  125.0 20.0 %all-gather.8.cloned.1.call-done = f32[256,64,128]{2,1,0:T(8,128)} async-done(((f32[16,64,128]{2,1,0:T(8,128)}), f32[256,64,128]{2,1,0:T(8,128)}) %all-gather.8.cloned.1.call-update) | async-done | bytes 8388624 | tf_op jit(solution)/shard_map/all_gather | solution.py:43
  145.1 28.2 %while.9 = (s32[]{:T(128)}, f32[16,64,128]{2,1,0:T(8,128)S(1)}, s32[]{:T(128)}, f32[16,16]{1,0:T(8,128)}, f32[16,16,64,128]{3,2,1,0:T(8,128)}, /*index=5*/s32[]{:T(128)}, s32[]{:T(128)}) while((s32[]{:T(128)}, f32[16,64,128]{2,1,0:T(8,128)S(1)}, s32[]{:T(128)}, f32[16,16]{1,0:T(8,128)}, f32[16,16,64,128]{3,2,1,0:T(8,128)}, ...), condition=%wide.region_4.5_spmd.clone, body=%wide.region_3.4_spmd.clone.sunk | while | flops 524292 | bytes 1573161 | solution.py:52
  186.5 7.5 %all-to-all-start = ((bf16[32,24,1024]{2,1,0:T(8,128)(2,1)}), bf16[32,24,1024]{2,1,0:T(8,128)(2,1)S(1)}, u32[]{:S(2)}, u32[]{:S(2)}) async-start(bf16[32,24,1024]{2,1,0:T(8,128)(2,1)} %bitcast.23), calls=%async_computation | async-start | bytes 3145728 | tf_op jit(solution)/shard_map/all_to_all | solution.py:153
  197.3 4.6 %collective-permute-start.13 = (bf16[64,1536]{1,0:T(8,128)(2,1)S(1)}, bf16[64,1536]{1,0:T(8,128)(2,1)S(1)}, u32[]{:S(2)}, u32[]{:S(2)}) collective-permute-start(bf16[64,1536]{1,0:T(8,128)(2,1)S(1)} %collective-permute-done.11), channel_id=1, source_target_pairs={{0,480},{32,0},{64,32},{96,64},{128,96},{160,128},{192,160},{224,1... | collective-permute-start | bytes 589832 | tf_op jit(solution)/shard_map/ppermute | solution.py:31
  203.3 5.8 %collective-permute-done.12 = bf16[64,1536]{1,0:T(8,128)(2,1)S(1)} collective-permute-done((bf16[64,1536]{1,0:T(8,128)(2,1)S(1)}, bf16[64,1536]{1,0:T(8,128)(2,1)S(1)}, u32[]{:S(2)}, u32[]{:S(2)}) %collective-permute-start.12) | collective-permute-done | bytes 196640 | tf_op jit(solution)/shard_map/ppermute | solution.py:23
  212.4 7.1 %collective-permute-done.14 = bf16[64,1536]{1,0:T(8,128)(2,1)S(1)} collective-permute-done((bf16[64,1536]{1,0:T(8,128)(2,1)S(1)}, bf16[64,1536]{1,0:T(8,128)(2,1)S(1)}, u32[]{:S(2)}, u32[]{:S(2)}) %collective-permute-start.14) | collective-permute-done | bytes 196640 | tf_op jit(solution)/shard_map/ppermute | solution.py:23
  220.2 6.1 %fusion.9 = f32[768,1536]{1,0:T(8,128)} fusion(bf16[768,1024]{1,0:T(8,128)(2,1)S(1)} %bitcast.162, bf16[1,1024,1536]{2,1,0:T(8,128)(2,1)} %all-gather.10.cloned.1.call-done), kind=kOutput, calls=%fused_computation.14 | convolution fusion | flops 2415919104 | bytes 9437184 | tf_op jit(solution)/shard_map/dot_general | solution.py:163
  226.2 62.8 %all-gather.12.cloned.1.call-done = bf16[1,1536,1024]{2,1,0:T(8,128)(2,1)} async-done(((bf16[1,96,1024]{2,1,0:T(8,128)(2,1)}), bf16[1,1536,1024]{2,1,0:T(8,128)(2,1)}) %all-gather.12.cloned.1.call-update) | async-done | bytes 3145744 | tf_op jit(solution)/shard_map/all_gather | solution.py:173
  289.0 10.5 %fusion.16 = bf16[768,1024]{1,0:T(8,128)(2,1)} fusion(bf16[1,1536,1024]{2,1,0:T(8,128)(2,1)} %all-gather.12.cloned.1.call-done, f32[768,1536]{1,0:T(8,128)} %fusion.9, bf16[768,1024]{1,0:T(8,128)(2,1)S(1)} %bitcast.163, bf16[1024,1536]{1,0:T(8,128)(2,1)} %constant_dynamic-update-slice_fusion), kind=kOutput, calls=%fused_computation.21 | convolution fusion | flops 4839702528 | bytes 14155776 | tf_op jit(solution)/shard_map/dot_general | solution.py:171
  299.5 16.2 %all-to-all-start.1 = ((bf16[32,24,1024]{2,1,0:T(8,128)(2,1)}), bf16[32,24,1024]{2,1,0:T(8,128)(2,1)S(1)}, u32[]{:S(2)}, u32[]{:S(2)}) async-start(bf16[32,24,1024]{2,1,0:T(8,128)(2,1)} %bitcast.164), calls=%async_computation.1 | async-start | bytes 3145728 | tf_op jit(solution)/shard_map/all_to_all | solution.py:176
  318.3 20.1 %all-to-all-done.1 = bf16[32,24,1024]{2,1,0:T(8,128)(2,1)S(1)} async-done(((bf16[32,24,1024]{2,1,0:T(8,128)(2,1)}), bf16[32,24,1024]{2,1,0:T(8,128)(2,1)S(1)}, u32[]{:S(2)}, u32[]{:S(2)}) %all-to-all-start.1) | async-done | bytes 1572896 | tf_op jit(solution)/shard_map/all_to_all | solution.py:176
  (152 shorter events, 93.3 us)
Async XLA Ops:
  6.5 47.9 %copy-start = (f32[1,256,128]{2,1,0:T(8,128)S(1)}, f32[1,256,128]{2,1,0:T(8,128)}, u32[]{:S(2)}) copy-start(f32[1,256,128]{2,1,0:T(8,128)} %param.19) | copy-start | bytes 393220
  6.5 138.5 %all-gather.8.cloned.1.call-start = ((), (), s32[]{:S(2)}) async-start(), calls=%async_computation.2 | async-start | bytes 8912896 | tf_op jit(solution)/shard_map/all_gather | solution.py:43
  8.5 18.5 %copy-start.7 = (f32[1,256,16]{1,2,0:T(8,128)S(1)}, f32[1,256,16]{1,2,0:T(8,128)}, u32[]{:S(2)}) copy-start(f32[1,256,16]{1,2,0:T(8,128)} %param.20) | copy-start | bytes 49156
  10.1 17.1 %copy-start.10 = (s32[1,256,2]{1,2,0:T(2,128)S(1)}, s32[1,256,2]{1,2,0:T(2,128)}, u32[]{:S(2)}) copy-start(s32[1,256,2]{1,2,0:T(2,128)} %param.28) | copy-start | bytes 6148
  10.1 44.7 %copy-start.1 = (bf16[1,256,1024]{2,1,0:T(8,128)(2,1)S(1)}, bf16[1,256,1024]{2,1,0:T(8,128)(2,1)}, u32[]{:S(2)}) copy-start(bf16[1,256,1024]{2,1,0:T(8,128)(2,1)} %param.17) | copy-start | bytes 1572868
  12.0 208.2 %all-gather.10.cloned.1.call-start = ((), (), s32[]{:S(2)}) async-start(), calls=%async_computation.3 | async-start | bytes 3342336 | tf_op jit(solution)/shard_map/all_gather | solution.py:165
  12.8 276.3 %all-gather.12.cloned.1.call-start = ((), (), s32[]{:S(2)}) async-start(), calls=%async_computation.4 | async-start | bytes 3342336 | tf_op jit(solution)/shard_map/all_gather | solution.py:173
  12.8 55.4 %collective-permute-start = (bf16[64,1536]{1,0:T(8,128)(2,1)S(1)}, bf16[64,1536]{1,0:T(8,128)(2,1)S(1)}, u32[]{:S(2)}, u32[]{:S(2)}) collective-permute-start(bf16[64,1536]{1,0:T(8,128)(2,1)S(1)} %bitcast.167), channel_id=1, source_target_pairs={{0,32},{32,64},{64,96},{96,128},{128,160},{160,192},{192,224},{224... | collective-permute-start | bytes 589832 | tf_op jit(solution)/shard_map/ppermute | solution.py:23
  17.2 52.9 %collective-permute-start.1 = (bf16[64,1536]{1,0:T(8,128)(2,1)S(1)}, bf16[64,1536]{1,0:T(8,128)(2,1)S(1)}, u32[]{:S(2)}, u32[]{:S(2)}) collective-permute-start(bf16[64,1536]{1,0:T(8,128)(2,1)S(1)} %bitcast.168), channel_id=1, source_target_pairs={{0,480},{32,0},{64,32},{96,64},{128,96},{160,128},{192,160},{224,1... | collective-permute-start | bytes 589832 | tf_op jit(solution)/shard_map/ppermute | solution.py:31
  68.2 12.2 %collective-permute-start.2 = (bf16[64,1536]{1,0:T(8,128)(2,1)S(1)}, bf16[64,1536]{1,0:T(8,128)(2,1)S(1)}, u32[]{:S(2)}, u32[]{:S(2)}) collective-permute-start(bf16[64,1536]{1,0:T(8,128)(2,1)S(1)} %collective-permute-done), channel_id=1, source_target_pairs={{0,32},{32,64},{64,96},{96,128},{128,160},{160,192},{192,224},{224... | collective-permute-start | bytes 589832 | tf_op jit(solution)/shard_map/ppermute | solution.py:23
  70.1 12.2 %collective-permute-start.3 = (bf16[64,1536]{1,0:T(8,128)(2,1)S(1)}, bf16[64,1536]{1,0:T(8,128)(2,1)S(1)}, u32[]{:S(2)}, u32[]{:S(2)}) collective-permute-start(bf16[64,1536]{1,0:T(8,128)(2,1)S(1)} %collective-permute-done.1), channel_id=1, source_target_pairs={{0,480},{32,0},{64,32},{96,64},{128,96},{160,128},{192,160},{224,1... | collective-permute-start | bytes 589832 | tf_op jit(solution)/shard_map/ppermute | solution.py:31
  80.4 12.4 %collective-permute-start.4 = (bf16[64,1536]{1,0:T(8,128)(2,1)S(1)}, bf16[64,1536]{1,0:T(8,128)(2,1)S(1)}, u32[]{:S(2)}, u32[]{:S(2)}) collective-permute-start(bf16[64,1536]{1,0:T(8,128)(2,1)S(1)} %collective-permute-done.2), channel_id=1, source_target_pairs={{0,32},{32,64},{64,96},{96,128},{128,160},{160,192},{192,224},{224... | collective-permute-start | bytes 589832 | tf_op jit(solution)/shard_map/ppermute | solution.py:23
  82.3 12.4 %collective-permute-start.5 = (bf16[64,1536]{1,0:T(8,128)(2,1)S(1)}, bf16[64,1536]{1,0:T(8,128)(2,1)S(1)}, u32[]{:S(2)}, u32[]{:S(2)}) collective-permute-start(bf16[64,1536]{1,0:T(8,128)(2,1)S(1)} %collective-permute-done.3), channel_id=1, source_target_pairs={{0,480},{32,0},{64,32},{96,64},{128,96},{160,128},{192,160},{224,1... | collective-permute-start | bytes 589832 | tf_op jit(solution)/shard_map/ppermute | solution.py:31
  92.8 12.7 %collective-permute-start.6 = (bf16[64,1536]{1,0:T(8,128)(2,1)S(1)}, bf16[64,1536]{1,0:T(8,128)(2,1)S(1)}, u32[]{:S(2)}, u32[]{:S(2)}) collective-permute-start(bf16[64,1536]{1,0:T(8,128)(2,1)S(1)} %collective-permute-done.4), channel_id=1, source_target_pairs={{0,32},{32,64},{64,96},{96,128},{128,160},{160,192},{192,224},{224... | collective-permute-start | bytes 589832 | tf_op jit(solution)/shard_map/ppermute | solution.py:23
  94.7 12.6 %collective-permute-start.7 = (bf16[64,1536]{1,0:T(8,128)(2,1)S(1)}, bf16[64,1536]{1,0:T(8,128)(2,1)S(1)}, u32[]{:S(2)}, u32[]{:S(2)}) collective-permute-start(bf16[64,1536]{1,0:T(8,128)(2,1)S(1)} %collective-permute-done.5), channel_id=1, source_target_pairs={{0,480},{32,0},{64,32},{96,64},{128,96},{160,128},{192,160},{224,1... | collective-permute-start | bytes 589832 | tf_op jit(solution)/shard_map/ppermute | solution.py:31
  105.4 12.9 %collective-permute-start.8 = (bf16[64,1536]{1,0:T(8,128)(2,1)S(1)}, bf16[64,1536]{1,0:T(8,128)(2,1)S(1)}, u32[]{:S(2)}, u32[]{:S(2)}) collective-permute-start(bf16[64,1536]{1,0:T(8,128)(2,1)S(1)} %collective-permute-done.6), channel_id=1, source_target_pairs={{0,32},{32,64},{64,96},{96,128},{128,160},{160,192},{192,224},{224... | collective-permute-start | bytes 589832 | tf_op jit(solution)/shard_map/ppermute | solution.py:23
  107.4 12.9 %collective-permute-start.9 = (bf16[64,1536]{1,0:T(8,128)(2,1)S(1)}, bf16[64,1536]{1,0:T(8,128)(2,1)S(1)}, u32[]{:S(2)}, u32[]{:S(2)}) collective-permute-start(bf16[64,1536]{1,0:T(8,128)(2,1)S(1)} %collective-permute-done.7), channel_id=1, source_target_pairs={{0,480},{32,0},{64,32},{96,64},{128,96},{160,128},{192,160},{224,1... | collective-permute-start | bytes 589832 | tf_op jit(solution)/shard_map/ppermute | solution.py:31
  118.4 77.0 %collective-permute-start.10 = (bf16[64,1536]{1,0:T(8,128)(2,1)S(1)}, bf16[64,1536]{1,0:T(8,128)(2,1)S(1)}, u32[]{:S(2)}, u32[]{:S(2)}) collective-permute-start(bf16[64,1536]{1,0:T(8,128)(2,1)S(1)} %collective-permute-done.8), channel_id=1, source_target_pairs={{0,32},{32,64},{64,96},{96,128},{128,160},{160,192},{192,224},{224... | collective-permute-start | bytes 589832 | tf_op jit(solution)/shard_map/ppermute | solution.py:23
  120.3 77.0 %collective-permute-start.11 = (bf16[64,1536]{1,0:T(8,128)(2,1)S(1)}, bf16[64,1536]{1,0:T(8,128)(2,1)S(1)}, u32[]{:S(2)}, u32[]{:S(2)}) collective-permute-start(bf16[64,1536]{1,0:T(8,128)(2,1)S(1)} %collective-permute-done.9), channel_id=1, source_target_pairs={{0,480},{32,0},{64,32},{96,64},{128,96},{160,128},{192,160},{224,1... | collective-permute-start | bytes 589832 | tf_op jit(solution)/shard_map/ppermute | solution.py:31
  186.5 33.7 %all-to-all-start = ((bf16[32,24,1024]{2,1,0:T(8,128)(2,1)}), bf16[32,24,1024]{2,1,0:T(8,128)(2,1)S(1)}, u32[]{:S(2)}, u32[]{:S(2)}) async-start(bf16[32,24,1024]{2,1,0:T(8,128)(2,1)} %bitcast.23), calls=%async_computation | async-start | bytes 3145728 | tf_op jit(solution)/shard_map/all_to_all | solution.py:153
  195.4 13.7 %collective-permute-start.12 = (bf16[64,1536]{1,0:T(8,128)(2,1)S(1)}, bf16[64,1536]{1,0:T(8,128)(2,1)S(1)}, u32[]{:S(2)}, u32[]{:S(2)}) collective-permute-start(bf16[64,1536]{1,0:T(8,128)(2,1)S(1)} %collective-permute-done.10), channel_id=1, source_target_pairs={{0,32},{32,64},{64,96},{96,128},{128,160},{160,192},{192,224},{224... | collective-permute-start | bytes 589832 | tf_op jit(solution)/shard_map/ppermute | solution.py:23
  197.3 14.4 %collective-permute-start.13 = (bf16[64,1536]{1,0:T(8,128)(2,1)S(1)}, bf16[64,1536]{1,0:T(8,128)(2,1)S(1)}, u32[]{:S(2)}, u32[]{:S(2)}) collective-permute-start(bf16[64,1536]{1,0:T(8,128)(2,1)S(1)} %collective-permute-done.11), channel_id=1, source_target_pairs={{0,480},{32,0},{64,32},{96,64},{128,96},{160,128},{192,160},{224,1... | collective-permute-start | bytes 589832 | tf_op jit(solution)/shard_map/ppermute | solution.py:31
  209.1 10.4 %collective-permute-start.14 = (bf16[64,1536]{1,0:T(8,128)(2,1)S(1)}, bf16[64,1536]{1,0:T(8,128)(2,1)S(1)}, u32[]{:S(2)}, u32[]{:S(2)}) collective-permute-start(bf16[64,1536]{1,0:T(8,128)(2,1)S(1)} %collective-permute-done.12), channel_id=1, source_target_pairs={{0,32},{32,64},{64,96},{96,128},{128,160},{160,192},{192,224},{224... | collective-permute-start | bytes 589832 | tf_op jit(solution)/shard_map/ppermute | solution.py:23
  299.5 38.9 %all-to-all-start.1 = ((bf16[32,24,1024]{2,1,0:T(8,128)(2,1)}), bf16[32,24,1024]{2,1,0:T(8,128)(2,1)S(1)}, u32[]{:S(2)}, u32[]{:S(2)}) async-start(bf16[32,24,1024]{2,1,0:T(8,128)(2,1)} %bitcast.164), calls=%async_computation.1 | async-start | bytes 3145728 | tf_op jit(solution)/shard_map/all_to_all | solution.py:176
  (11 other events, 55.0 us)
Sparse Core Ops, SparseCore 0:
  12.1 132.8 all-gather.7
  147.1 68.2 all-gather.9
  217.5 71.5 all-gather.11
